TPU v7x, 32 devices: a whole 2x2x4 slice. The times are simulated.
32 devices in a mesh: band: 8 (over y, x, core), lev: 4 (over z).
Axes of the slice: x: 2, y: 2, z: 4, core: 2. Of those that a mesh axis runs over, the one named last changes fastest.
Arguments:
- spectral: bfloat16 [2, 2, 4, 1280, 2561], P(None, None, 'lev', 'band'), may hold values from -0.005859375 to 0.005859375
- legendre: bfloat16 [1280, 8, 2561], P('band'), may hold values from -6 to 6
- cycle_len: int32 [8], replicated, may hold values from 20 to 10256, as said below
- pair_wave: int32 [1280], replicated, may hold values from 0 to 1279, each once
- quad_weight: float32 [8], replicated, may hold values from 2 to 20
- forcing: bfloat16 [2, 4, 8, 10256], P(None, None, 'band', 'lev'), may hold values from -6 to 6
- mixing: bfloat16 [2, 4, 4], replicated, may hold values from -3 to 3
Outputs:
- tendency: bfloat16 [2, 2, 4, 1280, 2561], P(None, None, 'lev', 'band')
Inputs may be any that keep to these rules, and one draw needn't show every extreme that they name: `cycle_len`: each length is 20 + 4 i for distinct cycle numbers i from 0 to 2559; the cycle of length 10256 is present in every draw. `pair_wave`: each number from 0 to 1279 appears once.
All inputs are finite; a program needn't handle non-finite values.
Results may differ from a plain program's by a relative error of at most 0.008.
Values may be sent and summed in bfloat16 or wider, within the bound.
A program may use at most 128 MiB of HBM per device.

v0:
```python
import functools

import jax
import jax.numpy as jnp
from jax import lax
from jax.experimental import pallas as pl
from jax.experimental.pallas import tpu as pltpu
from jax.sharding import PartitionSpec as P

TRUNC = 2559
FIELDS = 2
INNER = 256
TWO_PI = 6.283185307179586


def pair_block(pair_dev):
    return 16 if pair_dev % 16 == 0 else 8


def sincos(wave, point, length, inverse_length):
    number = wave * point
    turns = jnp.floor(number.astype(jnp.float32) * inverse_length).astype(jnp.int32)
    residue = (number - turns * length).astype(jnp.float32) * inverse_length
    quarter = jnp.floor(residue * 4.0 + 0.5)
    t = (residue - quarter * 0.25) * TWO_PI
    t2 = t * t
    sin_t = t * (1.0 + t2 * (-1.0 / 6 + t2 * (1.0 / 120 + t2 * (-1.0 / 5040 + t2 * (1.0 / 362880)))))
    cos_t = 1.0 + t2 * (
        -0.5 + t2 * (1.0 / 24 + t2 * (-1.0 / 720 + t2 * (1.0 / 40320 + t2 * (-1.0 / 3628800))))
    )
    q = quarter.astype(jnp.int32)
    swap = (q & 1) == 1
    cos_v = jnp.where(swap, sin_t, cos_t)
    sin_v = jnp.where(swap, cos_t, sin_t)
    cos_v = jnp.where(((q + 1) & 2) == 2, -cos_v, cos_v)
    sin_v = jnp.where((q & 2) == 2, -sin_v, sin_v)
    return cos_v, sin_v


def diagonal(pairs, cycles):
    rows = lax.broadcasted_iota(jnp.int32, (pairs, cycles, 8 * pairs), 0)
    lanes = lax.broadcasted_iota(jnp.int32, (pairs, cycles, 8 * pairs), 2) % pairs
    return rows == lanes


def read_chunk(leg_hbm, leg_vmem, sem, pairs, i):
    part = pl.ds(pl.multiple_of(i * pairs, pairs), pairs)
    return pltpu.make_async_copy(leg_hbm.at[part], leg_vmem.at[part], sem.at[i])


def direct_kernel(split, limit_ref, coeff_ref, leg_hbm, out_hbm, leg_vmem, out_vmem, in_sem, out_sem):
    blocks, cycles, wide_lanes = coeff_ref.shape
    pairs = wide_lanes // 8
    packed = leg_vmem.shape[2]

    def write(i):
        part = pl.ds(pl.multiple_of(i * pairs, pairs), pairs)
        return pltpu.make_async_copy(
            out_vmem.at[:, :, :, part], out_hbm.at[:, :, :, part], out_sem.at[i]
        )

    for i in range(blocks):
        read_chunk(leg_hbm, leg_vmem, in_sem, pairs, i).start()
    mask = diagonal(pairs, cycles)
    column = split + lax.broadcasted_iota(jnp.int32, (pairs, packed - split), 1)
    half = 4 * pairs

    @pl.loop(0, blocks)
    def _(i):
        part = pl.ds(pl.multiple_of(i * pairs, pairs), pairs)
        wide = jnp.broadcast_to(coeff_ref[pl.ds(i, 1)], (pairs, cycles, 8 * pairs))
        wide = jnp.where(mask, wide, 0.0).reshape(pairs * cycles, 8 * pairs)
        wide = wide.T.astype(jnp.bfloat16)
        lower = column < limit_ref[part]
        read_chunk(leg_hbm, leg_vmem, in_sem, pairs, i).wait()
        leg = leg_vmem[part].reshape(pairs * cycles, packed)
        left = jnp.dot(wide[:half], leg[:, :split], preferred_element_type=jnp.float32)
        right = jnp.dot(wide, leg[:, split:], preferred_element_type=jnp.float32)
        for s in range(2):
            for f in range(FIELDS):
                at = (s * FIELDS + f) * pairs
                out_vmem[s, f, 0, part, :split] = left[at : at + pairs].astype(jnp.bfloat16)
                low, high = right[at : at + pairs], right[half + at : half + at + pairs]
                out_vmem[s, f, 0, part, split:] = jnp.where(lower, low, high).astype(jnp.bfloat16)
        write(i).start()

    for i in range(blocks):
        write(i).wait()


def grid_kernel(
    points_dev, levs, split, length_ref, weight_ref, low_ref, forcing_ref, mixing_ref, spec_hbm, leg_hbm,
    out_ref, limit_ref,
    cos_tab, sin_tab, cos_out, sin_out, twist_re, twist_im,
    outgoing, incoming, partial, arrived, leg_vmem, spec_vmem, four_ref, wave_ref,
    send_sem, recv_sem, send_back, recv_back, leg_sem, spec_sem,
):
    blocks, cycles, wide = four_ref.shape
    pairs = wide // 8
    packed = leg_vmem.shape[2]
    each = wide // 4

    def read_spec(i):
        part = pl.ds(pl.multiple_of(i * pairs, pairs), pairs)
        return pltpu.make_async_copy(
            spec_hbm.at[:, :, :, part], spec_vmem.at[:, :, :, part], spec_sem.at[i]
        )

    for i in range(blocks):
        read_spec(i).start()
        read_chunk(leg_hbm, leg_vmem, leg_sem, pairs, i).start()
    rows = FIELDS * levs
    outer = cos_out.shape[0]
    used = pl.cdiv(points_dev, INNER)
    slots, _, lanes = incoming.shape
    bands = slots // levs
    band_id = lax.axis_index("band")
    lev_id = lax.axis_index("lev")
    me = band_id * levs + lev_id
    length = length_ref[band_id]
    base = lev_id * points_dev
    inverse_length = 1.0 / jnp.full((1, lanes), length, jnp.int32).astype(jnp.float32)
    factor = inverse_length * weight_ref[band_id]

    barrier = pltpu.get_barrier_semaphore()

    def other(step):
        peer = (me + step) % slots
        return peer // levs, peer % levs

    @pl.loop(1, slots)
    def _(step):
        band, lev = other(step)
        pl.semaphore_signal(
            barrier, inc=1, device_id={"band": band, "lev": lev}, device_id_type=pl.DeviceIdType.MESH
        )

    own = blocks * pairs
    line = low_ref[...].reshape(1, bands * own)
    low = jnp.concatenate([line[:, k * own : (k + 1) * own] for k in range(bands)], axis=0)
    parts = [low, TRUNC - low]
    if lanes > blocks * each:
        parts.append(jnp.full((bands, lanes - blocks * each), 1 << 14, jnp.int32))
    wave_ref[...] = jnp.concatenate(parts, axis=1)
    mine = jnp.broadcast_to(wave_ref[pl.ds(band_id, 1), :].astype(jnp.float32), (8, lanes)).T
    limit_ref[...] = TRUNC + 1 - mine[: blocks * pairs, 0:1].astype(jnp.int32)

    def tables(c):
        span = pl.ds(pl.multiple_of(c * lanes, lanes), lanes)
        wave = wave_ref[pl.ds(c, 1), :]
        eight = lax.broadcasted_iota(jnp.int32, (8, lanes), 0)
        c0, s0 = sincos(wave, eight, length, inverse_length)
        c1, s1 = sincos(wave, eight * 8, length, inverse_length)
        c2, s2 = sincos(wave, eight * 64, length, inverse_length)
        steps = lax.broadcasted_iota(jnp.int32, (outer, lanes), 0)
        c3, s3 = sincos(wave, base + steps * INNER, length, inverse_length)
        cos_out[:, span] = c3
        sin_out[:, span] = s3
        for high in range(INNER // 64):
            ch, sh = c2[high : high + 1], s2[high : high + 1]
            for mid in range(8):
                cm, sm = c1[mid : mid + 1], s1[mid : mid + 1]
                cj, sj = ch * cm - sh * sm, ch * sm + sh * cm
                at = high * 64 + mid * 8
                cos_tab[at : at + 8, span] = (c0 * cj - s0 * sj).astype(jnp.bfloat16)
                sin_tab[at : at + 8, span] = (s0 * cj + c0 * sj).astype(jnp.bfloat16)

    early = bands // 2
    pl.loop(0, early)(tables)
    mask = diagonal(pairs, cycles)
    column = split + lax.broadcasted_iota(jnp.int32, (pairs, packed - split), 1)
    inner = (((1,), (1,)), ((), ()))

    @pl.loop(0, blocks)
    def _(i):
        part = pl.ds(pl.multiple_of(i * pairs, pairs), pairs)
        lower = column < limit_ref[part]
        read_spec(i).wait()
        whole, lows, highs = [], [], []
        for s in range(2):
            for f in range(FIELDS):
                whole.append(spec_vmem[s, f, 0, part, :split])
                row = spec_vmem[s, f, 0, part, split:].astype(jnp.float32)
                lows.append(jnp.where(lower, row, 0.0))
                highs.append(jnp.where(lower, 0.0, row))
        left = jnp.concatenate(whole, axis=0)
        right = jnp.concatenate(lows + highs, axis=0).astype(jnp.bfloat16)
        read_chunk(leg_hbm, leg_vmem, leg_sem, pairs, i).wait()
        leg = leg_vmem[part].reshape(pairs * cycles, packed)
        full = lax.dot_general(leg[:, split:], right, inner, preferred_element_type=jnp.float32)
        some = lax.dot_general(leg[:, :split], left, inner, preferred_element_type=jnp.float32)
        full = full + jnp.concatenate([some, jnp.zeros_like(some)], axis=1)
        full = full.reshape(pairs, cycles, 8 * pairs)
        four_ref[i] = jnp.sum(jnp.where(mask, full, 0.0), axis=0)

    sides = []
    for k in range(4):
        parts = [
            four_ref[i, :, (4 * h + k) * pairs : (4 * h + k + 1) * pairs]
            for h in range(2)
            for i in range(blocks)
        ]
        if lanes > blocks * each:
            parts.append(jnp.zeros((cycles, lanes - blocks * each), jnp.float32))
        sides.append(jnp.concatenate(parts, axis=1))
    for j in range(cycles):
        block = jnp.concatenate([side[j : j + 1] for side in sides], axis=0)
        outgoing[j] = block.astype(jnp.bfloat16)

    pl.semaphore_wait(barrier, slots - 1)

    @pl.loop(1, slots)
    def _(step):
        band, lev = other(step)
        pltpu.make_async_remote_copy(
            src_ref=outgoing.at[band], dst_ref=incoming.at[me], send_sem=send_sem,
            recv_sem=recv_sem, device_id={"band": band, "lev": lev},
            device_id_type=pl.DeviceIdType.MESH,
        ).start()

    incoming[me] = outgoing[band_id]
    pl.loop(early, bands)(tables)

    def wait_all(semaphore, buffer):
        most = buffer.at[pl.ds(0, slots - 1)]
        pltpu.make_async_copy(most, most, semaphore).wait()

    wait_all(recv_sem, incoming)

    @pl.loop(0, bands)
    def _(c):
        span = pl.ds(pl.multiple_of(c * lanes, lanes), lanes)
        wave = wave_ref[pl.ds(c, 1), :]
        gain = jnp.where(wave == 0, 1.0, 2.0)
        live = 2 * wave < length
        cells = [incoming[c * levs + lev].astype(jnp.float32) for lev in range(levs)]
        order = [(f, lev) for f in range(FIELDS) for lev in range(levs)]
        re = jnp.concatenate([cells[lev][f : f + 1] for f, lev in order], axis=0)
        im = jnp.concatenate([cells[lev][FIELDS + f : FIELDS + f + 1] for f, lev in order], axis=0)
        re = jnp.where(live, re * gain, 0.0)
        im = jnp.where(live, im * gain, 0.0)
        for a in range(used):
            co, so = cos_out[a : a + 1, span], sin_out[a : a + 1, span]
            twist_re[a * rows : (a + 1) * rows, span] = (re * co - im * so).astype(jnp.bfloat16)
            twist_im[a * rows : (a + 1) * rows, span] = -(re * so + im * co).astype(jnp.bfloat16)

    contract = (((1,), (1,)), ((), ()))
    grid = lax.dot_general(
        twist_re[...], cos_tab[...], contract, preferred_element_type=jnp.float32
    ) + lax.dot_general(twist_im[...], sin_tab[...], contract, preferred_element_type=jnp.float32)
    lane = lax.broadcasted_iota(jnp.int32, (rows, INNER), 1)
    mixing = mixing_ref[...].astype(jnp.float32)
    updated = []
    for a in range(used):
        point = a * INNER + lane
        inside = (point < points_dev) & (base + point < length)
        cell = jnp.where(inside, grid[a * rows : (a + 1) * rows], 0.0)
        product = (cell[:levs] * cell[levs:]).astype(jnp.bfloat16).astype(jnp.float32)
        force = forcing_ref[:, a * INNER : min((a + 1) * INNER, points_dev)].astype(jnp.float32)
        if force.shape[1] < INNER:
            rest = jnp.zeros((rows, INNER - force.shape[1]), jnp.float32)
            force = jnp.concatenate([force, rest], axis=1)
        total = cell + force
        for l2 in range(levs):
            total = total + mixing[:, l2 : l2 + 1] * product[l2 : l2 + 1]
        updated.append(jnp.where(inside, total, 0.0))
    updated = jnp.concatenate(updated, axis=0).astype(jnp.bfloat16)

    def send_band(band):
        @pl.loop(0, levs)
        def _(lev):
            @pl.when((band != band_id) | (lev != lev_id))
            def _():
                pltpu.make_async_remote_copy(
                    src_ref=partial.at[band * levs + lev], dst_ref=arrived.at[me],
                    send_sem=send_back, recv_sem=recv_back, device_id={"band": band, "lev": lev},
                    device_id_type=pl.DeviceIdType.MESH,
                ).start()

    @pl.loop(0, bands)
    def _(c):
        span = pl.ds(pl.multiple_of(c * lanes, lanes), lanes)
        cos_part = jnp.dot(updated, cos_tab[:, span], preferred_element_type=jnp.float32)
        sin_part = jnp.dot(updated, sin_tab[:, span], preferred_element_type=jnp.float32)
        re = jnp.zeros((rows, lanes), jnp.float32)
        im = jnp.zeros((rows, lanes), jnp.float32)
        for a in range(used):
            co, so = cos_out[a : a + 1, span], sin_out[a : a + 1, span]
            cp, sp = cos_part[a * rows : (a + 1) * rows], sin_part[a * rows : (a + 1) * rows]
            re = re + (cp * co - sp * so)
            im = im + (cp * so + sp * co)
        keep = 2 * wave_ref[pl.ds(c, 1), :] < length
        re = jnp.where(keep, re * factor, 0.0)
        im = jnp.where(keep, im * -factor, 0.0)
        for lev in range(levs):
            picks = [side[f * levs + lev : f * levs + lev + 1] for side in (re, im) for f in range(FIELDS)]
            partial[c * levs + lev] = jnp.concatenate(picks, axis=0).astype(jnp.bfloat16)

        @pl.when(c > 0)
        def _():
            send_band(c - 1)

    arrived[me] = partial[me]
    send_band(bands - 1)
    wait_all(recv_back, arrived)
    sums = []
    for j in range(cycles):
        total = arrived[j * levs].astype(jnp.float32)
        for lev in range(1, levs):
            total = total + arrived[j * levs + lev].astype(jnp.float32)
        sums.append(total)
    for k in range(4):
        side = jnp.concatenate([total[k : k + 1] for total in sums], axis=0)
        for h in range(2):
            for i in range(blocks):
                at, lane = (4 * h + k) * pairs, (h * blocks + i) * pairs
                out_ref[i, :, at : at + pairs] = side[:, lane : lane + pairs]
    wait_all(send_sem, incoming)
    wait_all(send_back, arrived)


def on_device(spectral, legendre, cycle_len, pair_wave, quad_weight, forcing, mixing):
    band_count = lax.axis_size("band")
    lev_count = lax.axis_size("lev")
    pair_dev = spectral.shape[3]
    cycles = legendre.shape[1]
    levels, points_dev = forcing.shape[1], forcing.shape[3]
    rows = FIELDS * levels
    pairs = pair_block(pair_dev)
    blocks = pair_dev // pairs

    each_band = pl.cdiv(2 * pair_dev, 128) * 128
    waves = band_count * each_band
    used = pl.cdiv(points_dev, INNER)
    outer = pl.cdiv(used, 8) * 8
    force = forcing.reshape(rows, points_dev)
    vmem = pl.BlockSpec(memory_space=pltpu.VMEM)
    smem = pl.BlockSpec(memory_space=pltpu.SMEM)
    slots = band_count * lev_count
    message = pltpu.VMEM((slots, 2 * FIELDS, each_band), jnp.bfloat16)
    split = (TRUNC + 2 - pair_wave.shape[0]) // 128 * 128
    hbm = pl.BlockSpec(memory_space=pl.ANY)
    coeff, limit = pl.pallas_call(
        functools.partial(grid_kernel, points_dev, lev_count, split),
        in_specs=[smem, smem, vmem, vmem, vmem, hbm, hbm],
        out_specs=[vmem, vmem],
        out_shape=[
            jax.ShapeDtypeStruct((blocks, cycles, 8 * pairs), jnp.float32),
            jax.ShapeDtypeStruct((pair_dev, 1), jnp.int32),
        ],
        scratch_shapes=[
            pltpu.VMEM((INNER, waves), jnp.bfloat16),
            pltpu.VMEM((INNER, waves), jnp.bfloat16),
            pltpu.VMEM((outer, waves), jnp.float32),
            pltpu.VMEM((outer, waves), jnp.float32),
            pltpu.VMEM((used * rows, waves), jnp.bfloat16),
            pltpu.VMEM((used * rows, waves), jnp.bfloat16),
            pltpu.VMEM((cycles, 2 * FIELDS, each_band), jnp.bfloat16),
            message, message, message,
            pltpu.VMEM(legendre.shape, jnp.bfloat16),
            pltpu.VMEM(spectral.shape, jnp.bfloat16),
            pltpu.VMEM((blocks, cycles, 8 * pairs), jnp.float32),
            pltpu.VMEM((band_count, each_band), jnp.int32),
        ]
        + [pltpu.SemaphoreType.DMA] * 4
        + [pltpu.SemaphoreType.DMA((blocks,))] * 2,
        compiler_params=pltpu.CompilerParams(collective_id=0, has_side_effects=True),
    )(
        cycle_len, quad_weight, pair_wave, force,
        mixing.reshape(rows, levels), spectral, legendre,
    )
    return pl.pallas_call(
        functools.partial(direct_kernel, split),
        in_specs=[vmem, vmem, hbm],
        out_specs=hbm,
        out_shape=jax.ShapeDtypeStruct(spectral.shape, jnp.bfloat16),
        scratch_shapes=[
            pltpu.VMEM(legendre.shape, jnp.bfloat16),
            pltpu.VMEM(spectral.shape, jnp.bfloat16),
        ]
        + [pltpu.SemaphoreType.DMA((blocks,))] * 2,
    )(limit, coeff, legendre)


def solution(mesh):
    return jax.shard_map(
        on_device,
        mesh=mesh,
        in_specs=(
            P(None, None, "lev", "band", None),
            P("band", None, None),
            P(),
            P(),
            P(),
            P(None, None, "band", "lev"),
            P(),
        ),
        out_specs=P(None, None, "lev", "band", None),
        check_vma=False,
    )
```

profile of v0, /device:TPU:0, one launch (start us, length us, event | category | flops | bytes accessed | tf_op | source)
XLA Modules:
  0.0 30.3 jit_solution(6789300752920139797)
XLA Ops:
  0.0 1.4 %reshape.6.forcing_ref = bf16[8,2564]{1,0:T(8,128)(2,1)} reshape(bf16[2,4,1,2564]{3,1,2,0:T(4,128)(2,1)} %param.12) | data formatting | bytes 82048 | tf_op jit(solution)/shard_map/reshape | solution.py:336
  1.4 22.1 %shard_map.73 = (f32[10,8,128]{2,1,0:T(8,128)}, s32[160,1]{1,0:T(8,128)}) custom-call(s32[8]{0:T(128)} %length_ref.1, f32[8]{0:T(128)} %weight_ref.1, s32[1280]{0:T(1024)} %low_ref.1, bf16[8,2564]{1,0:T(8,128)(2,1)} %reshape.6.forcing_ref, bf16[8,4]{1,0:T(8,128)(2,1)} %bitcast.3, bf16[2,2,1,160,2561]{4,3,2,1,0:T(8,128)(2,1)} %spec_hbm.1, ...), custom_call_target="tpu_custom_call" | custom-call | tf_op jit(solution)/shard_map/pallas_call | solution.py:343
  23.5 6.8 %shard_map.74 = bf16[2,2,1,160,2561]{4,3,2,1,0:T(8,128)(2,1)} custom-call(s32[160,1]{1,0:T(8,128)} %get-tuple-element.7.limit_ref, f32[10,8,128]{2,1,0:T(8,128)} %get-tuple-element.8.coeff_ref, bf16[160,8,2561]{2,1,0:T(8,128)(2,1)} %leg_hbm.3), custom_call_target="tpu_custom_call" | custom-call | tf_op jit(solution)/shard_map/pallas_call | solution.py:372
where the time goes:
time: 30.6 us; the launch traced here: 30.3 us
  Pallas kernels  28.8 us (94%)
  local copies, waits for them, and re-layouts  1.42 us (5%)
    pallas_call x1, Pallas kernels, on_device(): pl.pallas_call(functools.partial(grid_kernel, points_dev, lev_count, spli...  22.1 us
    pallas_call x1, Pallas kernels, on_device(): pl.pallas_call(functools.partial(direct_kernel, split), in_specs=[vmem, v...  6.8 us
    reshape x1, local copies, waits for them, and re-layouts, on_device(): force = forcing.reshape(rows, points_dev)  1.42 us

commit v1 on v0

--- a/solution.py
+++ b/solution.py
@@ -10,6 +10,7 @@
 TRUNC = 2559
 FIELDS = 2
 INNER = 256
+VMEM_LIMIT = 32 << 20
 TWO_PI = 6.283185307179586
 
 
@@ -43,15 +44,20 @@
     return rows == lanes
 
 
-def read_chunk(leg_hbm, leg_vmem, sem, pairs, i):
-    part = pl.ds(pl.multiple_of(i * pairs, pairs), pairs)
-    return pltpu.make_async_copy(leg_hbm.at[part], leg_vmem.at[part], sem.at[i])
-
-
-def direct_kernel(split, limit_ref, coeff_ref, leg_hbm, out_hbm, leg_vmem, out_vmem, in_sem, out_sem):
+def toggled(index, flips, count):
+    if count & (count - 1):
+        return (index + flips) % count
+    result, bit = 0, 1
+    while bit < count:
+        result = result + (index // bit + flips // bit) % 2 * bit
+        bit *= 2
+    return result
+
+
+def direct_kernel(split, limit_ref, coeff_ref, leg_ref, out_hbm, out_vmem, out_sem):
     blocks, cycles, wide_lanes = coeff_ref.shape
     pairs = wide_lanes // 8
-    packed = leg_vmem.shape[2]
+    packed = leg_ref.shape[2]
 
     def write(i):
         part = pl.ds(pl.multiple_of(i * pairs, pairs), pairs)
@@ -59,8 +65,6 @@
             out_vmem.at[:, :, :, part], out_hbm.at[:, :, :, part], out_sem.at[i]
         )
 
-    for i in range(blocks):
-        read_chunk(leg_hbm, leg_vmem, in_sem, pairs, i).start()
     mask = diagonal(pairs, cycles)
     column = split + lax.broadcasted_iota(jnp.int32, (pairs, packed - split), 1)
     half = 4 * pairs
@@ -72,8 +76,7 @@
         wide = jnp.where(mask, wide, 0.0).reshape(pairs * cycles, 8 * pairs)
         wide = wide.T.astype(jnp.bfloat16)
         lower = column < limit_ref[part]
-        read_chunk(leg_hbm, leg_vmem, in_sem, pairs, i).wait()
-        leg = leg_vmem[part].reshape(pairs * cycles, packed)
+        leg = leg_ref[part].reshape(pairs * cycles, packed)
         left = jnp.dot(wide[:half], leg[:, :split], preferred_element_type=jnp.float32)
         right = jnp.dot(wide, leg[:, split:], preferred_element_type=jnp.float32)
         for s in range(2):
@@ -89,15 +92,16 @@
 
 
 def grid_kernel(
-    points_dev, levs, split, length_ref, weight_ref, low_ref, forcing_ref, mixing_ref, spec_hbm, leg_hbm,
-    out_ref, limit_ref,
-    cos_tab, sin_tab, cos_out, sin_out, twist_re, twist_im,
-    outgoing, incoming, partial, arrived, leg_vmem, spec_vmem, four_ref, wave_ref,
-    send_sem, recv_sem, send_back, recv_back, leg_sem, spec_sem,
+    points_dev, levs, split, length_hbm, weight_hbm, low_hbm, forcing_hbm, mixing_hbm, spec_hbm, leg_hbm,
+    out_ref, limit_ref, leg_ref,
+    length_ref, weight_ref, low_ref, forcing_ref, mixing_ref,
+    cos_tab, sin_tab, cos_out, sin_out, twist_re, twist_im, grid_ref,
+    outgoing, incoming, partial, arrived, spec_vmem, four_ref, wave_ref,
+    send_sem, recv_sem, send_back, recv_back, leg_sem, spec_sem, small_sem,
 ):
     blocks, cycles, wide = four_ref.shape
     pairs = wide // 8
-    packed = leg_vmem.shape[2]
+    packed = leg_ref.shape[2]
     each = wide // 4
 
     def read_spec(i):
@@ -106,9 +110,27 @@
             spec_hbm.at[:, :, :, part], spec_vmem.at[:, :, :, part], spec_sem.at[i]
         )
 
+    def read_leg(i):
+        part = pl.ds(pl.multiple_of(i * pairs, pairs), pairs)
+        return pltpu.make_async_copy(leg_hbm.at[part], leg_ref.at[part], leg_sem.at[i])
+
+    small = [
+        pltpu.make_async_copy(src, dst, small_sem.at[k])
+        for k, (src, dst) in enumerate(
+            (
+                (low_hbm, low_ref), (length_hbm, length_ref), (weight_hbm, weight_ref),
+                (forcing_hbm, forcing_ref), (mixing_hbm, mixing_ref),
+            )
+        )
+    ]
+    for copy in small[:3]:
+        copy.start()
     for i in range(blocks):
         read_spec(i).start()
-        read_chunk(leg_hbm, leg_vmem, leg_sem, pairs, i).start()
+        read_leg(i).start()
+    for copy in small[3:]:
+        copy.start()
+
     rows = FIELDS * levs
     outer = cos_out.shape[0]
     used = pl.cdiv(points_dev, INNER)
@@ -117,23 +139,35 @@
     band_id = lax.axis_index("band")
     lev_id = lax.axis_index("lev")
     me = band_id * levs + lev_id
+    base = lev_id * points_dev
+    barrier = pltpu.get_barrier_semaphore()
+
+    def each_peer(act):
+        def of_band(flips, skip):
+            band = toggled(band_id, flips, bands)
+            for turn in range(levs - 1, skip - 1, -1):
+                act(band, (lev_id + turn) % levs)
+
+        if slots <= 64:
+            for flips in range(bands - 1, 0, -1):
+                of_band(flips, 0)
+        else:
+            @pl.loop(1, bands)
+            def _(step):
+                of_band(bands - step, 0)
+        of_band(0, 1)
+
+    each_peer(
+        lambda band, lev: pl.semaphore_signal(
+            barrier, inc=1, device_id={"band": band, "lev": lev}, device_id_type=pl.DeviceIdType.MESH
+        )
+    )
+
+    for copy in small[:3]:
+        copy.wait()
     length = length_ref[band_id]
-    base = lev_id * points_dev
     inverse_length = 1.0 / jnp.full((1, lanes), length, jnp.int32).astype(jnp.float32)
     factor = inverse_length * weight_ref[band_id]
-
-    barrier = pltpu.get_barrier_semaphore()
-
-    def other(step):
-        peer = (me + step) % slots
-        return peer // levs, peer % levs
-
-    @pl.loop(1, slots)
-    def _(step):
-        band, lev = other(step)
-        pl.semaphore_signal(
-            barrier, inc=1, device_id={"band": band, "lev": lev}, device_id_type=pl.DeviceIdType.MESH
-        )
 
     own = blocks * pairs
     line = low_ref[...].reshape(1, bands * own)
@@ -158,24 +192,20 @@
         sin_out[:, span] = s3
         for high in range(INNER // 64):
             ch, sh = c2[high : high + 1], s2[high : high + 1]
+            cj, sj = ch * c1 - sh * s1, ch * s1 + sh * c1
             for mid in range(8):
-                cm, sm = c1[mid : mid + 1], s1[mid : mid + 1]
-                cj, sj = ch * cm - sh * sm, ch * sm + sh * cm
+                cm, sm = cj[mid : mid + 1], sj[mid : mid + 1]
                 at = high * 64 + mid * 8
-                cos_tab[at : at + 8, span] = (c0 * cj - s0 * sj).astype(jnp.bfloat16)
-                sin_tab[at : at + 8, span] = (s0 * cj + c0 * sj).astype(jnp.bfloat16)
-
-    early = bands // 2
-    pl.loop(0, early)(tables)
+                cos_tab[at : at + 8, span] = (c0 * cm - s0 * sm).astype(jnp.bfloat16)
+                sin_tab[at : at + 8, span] = (s0 * cm + c0 * sm).astype(jnp.bfloat16)
+
     mask = diagonal(pairs, cycles)
     column = split + lax.broadcasted_iota(jnp.int32, (pairs, packed - split), 1)
     inner = (((1,), (1,)), ((), ()))
 
-    @pl.loop(0, blocks)
-    def _(i):
+    def legendre(i):
         part = pl.ds(pl.multiple_of(i * pairs, pairs), pairs)
         lower = column < limit_ref[part]
-        read_spec(i).wait()
         whole, lows, highs = [], [], []
         for s in range(2):
             for f in range(FIELDS):
@@ -185,13 +215,28 @@
                 highs.append(jnp.where(lower, 0.0, row))
         left = jnp.concatenate(whole, axis=0)
         right = jnp.concatenate(lows + highs, axis=0).astype(jnp.bfloat16)
-        read_chunk(leg_hbm, leg_vmem, leg_sem, pairs, i).wait()
-        leg = leg_vmem[part].reshape(pairs * cycles, packed)
+        leg = leg_ref[part].reshape(pairs * cycles, packed)
         full = lax.dot_general(leg[:, split:], right, inner, preferred_element_type=jnp.float32)
         some = lax.dot_general(leg[:, :split], left, inner, preferred_element_type=jnp.float32)
         full = full + jnp.concatenate([some, jnp.zeros_like(some)], axis=1)
         full = full.reshape(pairs, cycles, 8 * pairs)
         four_ref[i] = jnp.sum(jnp.where(mask, full, 0.0), axis=0)
+
+    def arrive(i):
+        read_spec(i).wait()
+        read_leg(i).wait()
+
+    both = min(blocks, bands)
+    @pl.loop(0, both)
+    def _(i):
+        arrive(i)
+        legendre(i)
+        tables(i)
+
+    @pl.loop(both, blocks)
+    def _(i):
+        arrive(i)
+        legendre(i)
 
     sides = []
     for k in range(4):
@@ -209,26 +254,27 @@
 
     pl.semaphore_wait(barrier, slots - 1)
 
-    @pl.loop(1, slots)
-    def _(step):
-        band, lev = other(step)
-        pltpu.make_async_remote_copy(
-            src_ref=outgoing.at[band], dst_ref=incoming.at[me], send_sem=send_sem,
-            recv_sem=recv_sem, device_id={"band": band, "lev": lev},
-            device_id_type=pl.DeviceIdType.MESH,
-        ).start()
-
+    def send(source, target, here, there):
+        def act(band, lev):
+            pltpu.make_async_remote_copy(
+                src_ref=source(band, lev), dst_ref=target.at[me], send_sem=here,
+                recv_sem=there, device_id={"band": band, "lev": lev},
+                device_id_type=pl.DeviceIdType.MESH,
+            ).start()
+        return act
+
+    each_peer(send(lambda band, lev: outgoing.at[band], incoming, send_sem, recv_sem.at[band_id]))
     incoming[me] = outgoing[band_id]
-    pl.loop(early, bands)(tables)
-
-    def wait_all(semaphore, buffer):
-        most = buffer.at[pl.ds(0, slots - 1)]
+
+    pl.loop(both, bands)(tables)
+
+    def wait_all(semaphore, buffer, count):
+        most = buffer.at[pl.ds(0, count)]
         pltpu.make_async_copy(most, most, semaphore).wait()
 
-    wait_all(recv_sem, incoming)
-
-    @pl.loop(0, bands)
-    def _(c):
+    contract = (((1,), (1,)), ((), ()))
+
+    def synthesis(c, first):
         span = pl.ds(pl.multiple_of(c * lanes, lanes), lanes)
         wave = wave_ref[pl.ds(c, 1), :]
         gain = jnp.where(wave == 0, 1.0, 2.0)
@@ -241,22 +287,34 @@
         im = jnp.where(live, im * gain, 0.0)
         for a in range(used):
             co, so = cos_out[a : a + 1, span], sin_out[a : a + 1, span]
-            twist_re[a * rows : (a + 1) * rows, span] = (re * co - im * so).astype(jnp.bfloat16)
-            twist_im[a * rows : (a + 1) * rows, span] = -(re * so + im * co).astype(jnp.bfloat16)
-
-    contract = (((1,), (1,)), ((), ()))
-    grid = lax.dot_general(
-        twist_re[...], cos_tab[...], contract, preferred_element_type=jnp.float32
-    ) + lax.dot_general(twist_im[...], sin_tab[...], contract, preferred_element_type=jnp.float32)
+            twist_re[a * rows : (a + 1) * rows] = (re * co - im * so).astype(jnp.bfloat16)
+            twist_im[a * rows : (a + 1) * rows] = -(re * so + im * co).astype(jnp.bfloat16)
+        grid = lax.dot_general(
+            twist_re[...], cos_tab[:, span], contract, preferred_element_type=jnp.float32
+        ) + lax.dot_general(twist_im[...], sin_tab[:, span], contract, preferred_element_type=jnp.float32)
+        grid_ref[...] = grid if first else grid_ref[...] + grid
+
+    wait_all(recv_sem.at[band_id], incoming, levs - 1)
+    synthesis(band_id, True)
+
+    @pl.loop(1, bands)
+    def _(flips):
+        band = toggled(band_id, flips, bands)
+        wait_all(recv_sem.at[band], incoming, levs)
+        synthesis(band, False)
+
+    for copy in small[3:]:
+        copy.wait()
     lane = lax.broadcasted_iota(jnp.int32, (rows, INNER), 1)
-    mixing = mixing_ref[...].astype(jnp.float32)
+    mixing = jnp.concatenate([mixing_ref[f].astype(jnp.float32) for f in range(FIELDS)], axis=0)
     updated = []
     for a in range(used):
         point = a * INNER + lane
         inside = (point < points_dev) & (base + point < length)
-        cell = jnp.where(inside, grid[a * rows : (a + 1) * rows], 0.0)
+        cell = jnp.where(inside, grid_ref[a * rows : (a + 1) * rows], 0.0)
         product = (cell[:levs] * cell[levs:]).astype(jnp.bfloat16).astype(jnp.float32)
-        force = forcing_ref[:, a * INNER : min((a + 1) * INNER, points_dev)].astype(jnp.float32)
+        span = slice(a * INNER, min((a + 1) * INNER, points_dev))
+        force = jnp.concatenate([forcing_ref[f, :, span].astype(jnp.float32) for f in range(FIELDS)], axis=0)
         if force.shape[1] < INNER:
             rest = jnp.zeros((rows, INNER - force.shape[1]), jnp.float32)
             force = jnp.concatenate([force, rest], axis=1)
@@ -266,19 +324,11 @@
         updated.append(jnp.where(inside, total, 0.0))
     updated = jnp.concatenate(updated, axis=0).astype(jnp.bfloat16)
 
-    def send_band(band):
-        @pl.loop(0, levs)
-        def _(lev):
-            @pl.when((band != band_id) | (lev != lev_id))
-            def _():
-                pltpu.make_async_remote_copy(
-                    src_ref=partial.at[band * levs + lev], dst_ref=arrived.at[me],
-                    send_sem=send_back, recv_sem=recv_back, device_id={"band": band, "lev": lev},
-                    device_id_type=pl.DeviceIdType.MESH,
-                ).start()
-
-    @pl.loop(0, bands)
-    def _(c):
+    send_partial = send(
+        lambda band, lev: partial.at[band * levs + lev], arrived, send_back, recv_back
+    )
+
+    def analysis(c):
         span = pl.ds(pl.multiple_of(c * lanes, lanes), lanes)
         cos_part = jnp.dot(updated, cos_tab[:, span], preferred_element_type=jnp.float32)
         sin_part = jnp.dot(updated, sin_tab[:, span], preferred_element_type=jnp.float32)
@@ -296,13 +346,22 @@
             picks = [side[f * levs + lev : f * levs + lev + 1] for side in (re, im) for f in range(FIELDS)]
             partial[c * levs + lev] = jnp.concatenate(picks, axis=0).astype(jnp.bfloat16)
 
-        @pl.when(c > 0)
-        def _():
-            send_band(c - 1)
+    def send_band(flips, skip):
+        band = toggled(band_id, flips, bands)
+        for turn in range(levs - 1, skip - 1, -1):
+            send_partial(band, (lev_id + turn) % levs)
+
+    analysis(toggled(band_id, bands - 1, bands))
+
+    @pl.loop(1, bands)
+    def _(step):
+        analysis(toggled(band_id, bands - 1 - step, bands))
+        send_band(bands - step, 0)
 
     arrived[me] = partial[me]
-    send_band(bands - 1)
-    wait_all(recv_back, arrived)
+    send_band(0, 1)
+
+    wait_all(recv_back, arrived, slots - 1)
     sums = []
     for j in range(cycles):
         total = arrived[j * levs].astype(jnp.float32)
@@ -315,8 +374,8 @@
             for i in range(blocks):
                 at, lane = (4 * h + k) * pairs, (h * blocks + i) * pairs
                 out_ref[i, :, at : at + pairs] = side[:, lane : lane + pairs]
-    wait_all(send_sem, incoming)
-    wait_all(send_back, arrived)
+    wait_all(send_sem, incoming, slots - 1)
+    wait_all(send_back, arrived, slots - 1)
 
 
 def on_device(spectral, legendre, cycle_len, pair_wave, quad_weight, forcing, mixing):
@@ -333,53 +392,64 @@
     waves = band_count * each_band
     used = pl.cdiv(points_dev, INNER)
     outer = pl.cdiv(used, 8) * 8
-    force = forcing.reshape(rows, points_dev)
+    force = forcing.reshape(FIELDS, levels, points_dev)
     vmem = pl.BlockSpec(memory_space=pltpu.VMEM)
-    smem = pl.BlockSpec(memory_space=pltpu.SMEM)
     slots = band_count * lev_count
     message = pltpu.VMEM((slots, 2 * FIELDS, each_band), jnp.bfloat16)
     split = (TRUNC + 2 - pair_wave.shape[0]) // 128 * 128
-    hbm = pl.BlockSpec(memory_space=pl.ANY)
-    coeff, limit = pl.pallas_call(
+    hbm = pl.BlockSpec(memory_space=pltpu.HBM)
+    coeff, limit, leg = pl.pallas_call(
         functools.partial(grid_kernel, points_dev, lev_count, split),
-        in_specs=[smem, smem, vmem, vmem, vmem, hbm, hbm],
-        out_specs=[vmem, vmem],
+        in_specs=[hbm] * 7,
+        out_specs=[vmem] * 3,
         out_shape=[
-            jax.ShapeDtypeStruct((blocks, cycles, 8 * pairs), jnp.float32),
-            jax.ShapeDtypeStruct((pair_dev, 1), jnp.int32),
+            pltpu.VMEM((blocks, cycles, 8 * pairs), jnp.float32),
+            pltpu.VMEM((pair_dev, 1), jnp.int32),
+            pltpu.VMEM(legendre.shape, jnp.bfloat16),
         ],
         scratch_shapes=[
+            pltpu.SMEM(cycle_len.shape, jnp.int32),
+            pltpu.SMEM(quad_weight.shape, jnp.float32),
+            pltpu.VMEM(pair_wave.shape, jnp.int32),
+            pltpu.VMEM(force.shape, jnp.bfloat16),
+            pltpu.VMEM(mixing.shape, jnp.bfloat16),
             pltpu.VMEM((INNER, waves), jnp.bfloat16),
             pltpu.VMEM((INNER, waves), jnp.bfloat16),
             pltpu.VMEM((outer, waves), jnp.float32),
             pltpu.VMEM((outer, waves), jnp.float32),
-            pltpu.VMEM((used * rows, waves), jnp.bfloat16),
-            pltpu.VMEM((used * rows, waves), jnp.bfloat16),
+            pltpu.VMEM((used * rows, each_band), jnp.bfloat16),
+            pltpu.VMEM((used * rows, each_band), jnp.bfloat16),
+            pltpu.VMEM((used * rows, INNER), jnp.float32),
             pltpu.VMEM((cycles, 2 * FIELDS, each_band), jnp.bfloat16),
             message, message, message,
-            pltpu.VMEM(legendre.shape, jnp.bfloat16),
             pltpu.VMEM(spectral.shape, jnp.bfloat16),
             pltpu.VMEM((blocks, cycles, 8 * pairs), jnp.float32),
             pltpu.VMEM((band_count, each_band), jnp.int32),
-        ]
-        + [pltpu.SemaphoreType.DMA] * 4
-        + [pltpu.SemaphoreType.DMA((blocks,))] * 2,
-        compiler_params=pltpu.CompilerParams(collective_id=0, has_side_effects=True),
+            pltpu.SemaphoreType.DMA,
+            pltpu.SemaphoreType.DMA((band_count,)),
+            pltpu.SemaphoreType.DMA,
+            pltpu.SemaphoreType.DMA,
+            pltpu.SemaphoreType.DMA((blocks,)),
+            pltpu.SemaphoreType.DMA((blocks,)),
+            pltpu.SemaphoreType.DMA((5,)),
+        ],
+        compiler_params=pltpu.CompilerParams(
+            collective_id=0, has_side_effects=True, vmem_limit_bytes=VMEM_LIMIT
+        ),
     )(
-        cycle_len, quad_weight, pair_wave, force,
-        mixing.reshape(rows, levels), spectral, legendre,
+        *(
+            pltpu.with_memory_space_constraint(array, pltpu.HBM)
+            for array in (cycle_len, quad_weight, pair_wave, force, mixing, spectral, legendre)
+        )
     )
     return pl.pallas_call(
         functools.partial(direct_kernel, split),
-        in_specs=[vmem, vmem, hbm],
+        in_specs=[vmem, vmem, vmem],
         out_specs=hbm,
         out_shape=jax.ShapeDtypeStruct(spectral.shape, jnp.bfloat16),
-        scratch_shapes=[
-            pltpu.VMEM(legendre.shape, jnp.bfloat16),
-            pltpu.VMEM(spectral.shape, jnp.bfloat16),
-        ]
-        + [pltpu.SemaphoreType.DMA((blocks,))] * 2,
-    )(limit, coeff, legendre)
+        scratch_shapes=[pltpu.VMEM(spectral.shape, jnp.bfloat16), pltpu.SemaphoreType.DMA((blocks,))],
+        compiler_params=pltpu.CompilerParams(vmem_limit_bytes=VMEM_LIMIT),
+    )(limit, coeff, leg)
 
 
 def solution(mesh):

time: 30.6 us -> 27.9 us (0.912)
  local copies, waits for them, and re-layouts: 1.42 us -> 0 us
  Pallas kernels: 28.8 us -> 27.8 us
    pallas_call x1, Pallas kernels: 6.8 us -> 4.37 us  [on_device(): pl.pallas_call(functools.partial(direct_kernel, split), in_specs=[vmem, v...]
    reshape x1 -> x0, local copies, waits for them, and re-layouts: 1.42 us -> none  [on_device(): force = forcing.reshape(rows, points_dev)]
    pallas_call x1, Pallas kernels: 22.1 us -> 23.4 us  [on_device(): pl.pallas_call(functools.partial(grid_kernel, points_dev, lev_count, spli...]
where the time goes in v1:
time: 27.9 us; the launch traced here: 27.8 us
  Pallas kernels  27.8 us (100%)
    pallas_call x1, Pallas kernels, on_device(): pl.pallas_call(functools.partial(grid_kernel, points_dev, lev_count, spli...  23.4 us
    pallas_call x1, Pallas kernels, on_device(): pl.pallas_call(functools.partial(direct_kernel, split), in_specs=[vmem, v...  4.37 us

profile of v1, /device:TPU:0, one launch (start us, length us, event | category | flops | bytes accessed | tf_op | source)
XLA Modules:
  0.0 27.8 jit_solution(3816095895727674492)
XLA Ops:
  0.0 23.4 %shard_map.73 = (f32[10,8,128]{2,1,0:T(8,128)S(1)}, s32[160,1]{1,0:T(8,128)S(1)}, bf16[160,8,2561]{2,1,0:T(8,128)(2,1)S(1)}) custom-call(s32[8]{0:T(128)} %length_hbm.1, f32[8]{0:T(128)} %weight_hbm.1, s32[1280]{0:T(1024)} %low_hbm.1, bf16[2,4,2564]{2,1,0:T(4,128)(2,1)} %bitcast.1, bf16[2,4,4]{2,1,0:T(4,128)(2,1)} %mixing_hbm.1, ...), custom_call_target="tpu_custom_call" | custom-call | tf_op jit(solution)/shard_map/pallas_call | solution.py:401
  23.4 4.4 %shard_map.74 = bf16[2,2,1,160,2561]{4,3,2,1,0:T(8,128)(2,1)} custom-call(s32[160,1]{1,0:T(8,128)S(1)} %get-tuple-element.8.limit_ref, f32[10,8,128]{2,1,0:T(8,128)S(1)} %get-tuple-element.9.coeff_ref, bf16[160,8,2561]{2,1,0:T(8,128)(2,1)S(1)} %get-tuple-element.10.leg_ref), custom_call_target="tpu_custom_call" | custom-call | tf_op jit(solution)/shard_map/pallas_call | solution.py:445

commit v2 on v1

--- a/solution.py
+++ b/solution.py
@@ -69,7 +69,7 @@
     column = split + lax.broadcasted_iota(jnp.int32, (pairs, packed - split), 1)
     half = 4 * pairs
 
-    @pl.loop(0, blocks)
+    @pl.loop(0, blocks, unroll=blocks <= 10)
     def _(i):
         part = pl.ds(pl.multiple_of(i * pairs, pairs), pairs)
         wide = jnp.broadcast_to(coeff_ref[pl.ds(i, 1)], (pairs, cycles, 8 * pairs))
@@ -95,7 +95,7 @@
     points_dev, levs, split, length_hbm, weight_hbm, low_hbm, forcing_hbm, mixing_hbm, spec_hbm, leg_hbm,
     out_ref, limit_ref, leg_ref,
     length_ref, weight_ref, low_ref, forcing_ref, mixing_ref,
-    cos_tab, sin_tab, cos_out, sin_out, twist_re, twist_im, grid_ref,
+    cos_tab, sin_tab, cos_out, sin_out, grid_ref,
     outgoing, incoming, partial, arrived, spec_vmem, four_ref, wave_ref,
     send_sem, recv_sem, send_back, recv_back, leg_sem, spec_sem, small_sem,
 ):
@@ -125,11 +125,6 @@
     ]
     for copy in small[:3]:
         copy.start()
-    for i in range(blocks):
-        read_spec(i).start()
-        read_leg(i).start()
-    for copy in small[3:]:
-        copy.start()
 
     rows = FIELDS * levs
     outer = cos_out.shape[0]
@@ -163,7 +158,13 @@
         )
     )
 
-    for copy in small[:3]:
+    for i in range(blocks):
+        read_spec(i).start()
+        read_leg(i).start()
+    for copy in small[3:]:
+        copy.start()
+
+    for at, copy in enumerate(small[:3]):
         copy.wait()
     length = length_ref[band_id]
     inverse_length = 1.0 / jnp.full((1, lanes), length, jnp.int32).astype(jnp.float32)
@@ -226,17 +227,18 @@
         read_spec(i).wait()
         read_leg(i).wait()
 
-    both = min(blocks, bands)
-    @pl.loop(0, both)
-    def _(i):
-        arrive(i)
-        legendre(i)
-        tables(i)
-
-    @pl.loop(both, blocks)
-    def _(i):
-        arrive(i)
-        legendre(i)
+    group = 2 if blocks % 2 == 0 else 1
+    early = min(2, bands)
+
+    pl.loop(0, early)(tables)
+
+    @pl.loop(0, blocks // group)
+    def _(step):
+        first = step * group
+        for at in range(group):
+            arrive(first + at)
+        for at in range(group):
+            legendre(first + at)
 
     sides = []
     for k in range(4):
@@ -266,42 +268,68 @@
     each_peer(send(lambda band, lev: outgoing.at[band], incoming, send_sem, recv_sem.at[band_id]))
     incoming[me] = outgoing[band_id]
 
-    pl.loop(both, bands)(tables)
+    pl.loop(early, bands)(tables)
 
     def wait_all(semaphore, buffer, count):
         most = buffer.at[pl.ds(0, count)]
         pltpu.make_async_copy(most, most, semaphore).wait()
 
     contract = (((1,), (1,)), ((), ()))
-
-    def synthesis(c, first):
-        span = pl.ds(pl.multiple_of(c * lanes, lanes), lanes)
-        wave = wave_ref[pl.ds(c, 1), :]
+    near = 2 if bands % 2 == 0 else 1
+    groups = bands // near
+
+    def span_of(group):
+        return pl.ds(pl.multiple_of(group * (near * lanes), near * lanes), near * lanes)
+
+    def waves_of(group):
+        return jnp.concatenate([wave_ref[pl.ds(group * near + at, 1), :] for at in range(near)], axis=1)
+
+    def synthesis(group):
+        span, wave = span_of(group), waves_of(group)
         gain = jnp.where(wave == 0, 1.0, 2.0)
         live = 2 * wave < length
-        cells = [incoming[c * levs + lev].astype(jnp.float32) for lev in range(levs)]
+        cells = [
+            jnp.concatenate([incoming[(group * near + at) * levs + lev] for at in range(near)], axis=1)
+            for lev in range(levs)
+        ]
+        cells = [cell.astype(jnp.float32) for cell in cells]
         order = [(f, lev) for f in range(FIELDS) for lev in range(levs)]
         re = jnp.concatenate([cells[lev][f : f + 1] for f, lev in order], axis=0)
         im = jnp.concatenate([cells[lev][FIELDS + f : FIELDS + f + 1] for f, lev in order], axis=0)
         re = jnp.where(live, re * gain, 0.0)
         im = jnp.where(live, im * gain, 0.0)
+        twist_re, twist_im = [], []
         for a in range(used):
             co, so = cos_out[a : a + 1, span], sin_out[a : a + 1, span]
-            twist_re[a * rows : (a + 1) * rows] = (re * co - im * so).astype(jnp.bfloat16)
-            twist_im[a * rows : (a + 1) * rows] = -(re * so + im * co).astype(jnp.bfloat16)
-        grid = lax.dot_general(
-            twist_re[...], cos_tab[:, span], contract, preferred_element_type=jnp.float32
-        ) + lax.dot_general(twist_im[...], sin_tab[:, span], contract, preferred_element_type=jnp.float32)
-        grid_ref[...] = grid if first else grid_ref[...] + grid
-
-    wait_all(recv_sem.at[band_id], incoming, levs - 1)
-    synthesis(band_id, True)
-
-    @pl.loop(1, bands)
-    def _(flips):
-        band = toggled(band_id, flips, bands)
-        wait_all(recv_sem.at[band], incoming, levs)
-        synthesis(band, False)
+            twist_re.append(re * co - im * so)
+            twist_im.append(-(re * so + im * co))
+        twist_re = jnp.concatenate(twist_re, axis=0).astype(jnp.bfloat16)
+        twist_im = jnp.concatenate(twist_im, axis=0).astype(jnp.bfloat16)
+        return lax.dot_general(
+            twist_re, cos_tab[:, span], contract, preferred_element_type=jnp.float32
+        ) + lax.dot_general(twist_im, sin_tab[:, span], contract, preferred_element_type=jnp.float32)
+
+    def wait_group(flips, own):
+        group = toggled(band_id // near, flips, groups)
+        for at in range(near):
+            if own:
+                first = (band_id + at) % near
+                wait_all(recv_sem.at[group * near + first], incoming, levs - (at == 0))
+            else:
+                wait_all(recv_sem.at[group * near + at], incoming, levs)
+        return group
+
+    if groups <= 8:
+        these = [wait_group(flips, flips == 0) for flips in range(groups)]
+        grid = sum(synthesis(group) for group in these)
+    else:
+        grid_ref[...] = synthesis(wait_group(0, True))
+
+        @pl.loop(1, groups)
+        def _(flips):
+            grid_ref[...] += synthesis(wait_group(flips, False))
+
+        grid = grid_ref[...]
 
     for copy in small[3:]:
         copy.wait()
@@ -311,7 +339,7 @@
     for a in range(used):
         point = a * INNER + lane
         inside = (point < points_dev) & (base + point < length)
-        cell = jnp.where(inside, grid_ref[a * rows : (a + 1) * rows], 0.0)
+        cell = jnp.where(inside, grid[a * rows : (a + 1) * rows], 0.0)
         product = (cell[:levs] * cell[levs:]).astype(jnp.bfloat16).astype(jnp.float32)
         span = slice(a * INNER, min((a + 1) * INNER, points_dev))
         force = jnp.concatenate([forcing_ref[f, :, span].astype(jnp.float32) for f in range(FIELDS)], axis=0)
@@ -328,38 +356,49 @@
         lambda band, lev: partial.at[band * levs + lev], arrived, send_back, recv_back
     )
 
-    def analysis(c):
-        span = pl.ds(pl.multiple_of(c * lanes, lanes), lanes)
+    def analysis(flips):
+        group = toggled(band_id // near, flips, groups)
+        span = span_of(group)
         cos_part = jnp.dot(updated, cos_tab[:, span], preferred_element_type=jnp.float32)
         sin_part = jnp.dot(updated, sin_tab[:, span], preferred_element_type=jnp.float32)
-        re = jnp.zeros((rows, lanes), jnp.float32)
-        im = jnp.zeros((rows, lanes), jnp.float32)
+        re = jnp.zeros((rows, near * lanes), jnp.float32)
+        im = jnp.zeros((rows, near * lanes), jnp.float32)
         for a in range(used):
             co, so = cos_out[a : a + 1, span], sin_out[a : a + 1, span]
             cp, sp = cos_part[a * rows : (a + 1) * rows], sin_part[a * rows : (a + 1) * rows]
             re = re + (cp * co - sp * so)
             im = im + (cp * so + sp * co)
-        keep = 2 * wave_ref[pl.ds(c, 1), :] < length
-        re = jnp.where(keep, re * factor, 0.0)
-        im = jnp.where(keep, im * -factor, 0.0)
+        scale = jnp.concatenate([factor] * near, axis=1)
+        keep = 2 * waves_of(group) < length
+        re = jnp.where(keep, re * scale, 0.0)
+        im = jnp.where(keep, im * -scale, 0.0)
         for lev in range(levs):
             picks = [side[f * levs + lev : f * levs + lev + 1] for side in (re, im) for f in range(FIELDS)]
-            partial[c * levs + lev] = jnp.concatenate(picks, axis=0).astype(jnp.bfloat16)
-
-    def send_band(flips, skip):
-        band = toggled(band_id, flips, bands)
-        for turn in range(levs - 1, skip - 1, -1):
-            send_partial(band, (lev_id + turn) % levs)
-
-    analysis(toggled(band_id, bands - 1, bands))
-
-    @pl.loop(1, bands)
-    def _(step):
-        analysis(toggled(band_id, bands - 1 - step, bands))
-        send_band(bands - step, 0)
+            picks = jnp.concatenate(picks, axis=0).astype(jnp.bfloat16)
+            for at in range(near):
+                partial[(group * near + at) * levs + lev] = picks[:, at * lanes : (at + 1) * lanes]
+
+    def send_group(flips):
+        group = toggled(band_id // near, flips, groups)
+        for at in range(near - 1, -1, -1):
+            own = isinstance(flips, int) and flips == 0 and at == 0
+            band = group * near + (band_id + at) % near
+            for turn in range(levs - 1, 0 if own else -1, -1):
+                send_partial(band, (lev_id + turn) % levs)
+
+    analysis(groups - 1)
+    if groups <= 8:
+        for flips in range(groups - 2, -1, -1):
+            analysis(flips)
+            send_group(flips + 1)
+    else:
+        @pl.loop(1, groups)
+        def _(step):
+            analysis(groups - 1 - step)
+            send_group(groups - step)
 
     arrived[me] = partial[me]
-    send_band(0, 1)
+    send_group(0)
 
     wait_all(recv_back, arrived, slots - 1)
     sums = []
@@ -417,8 +456,6 @@
             pltpu.VMEM((INNER, waves), jnp.bfloat16),
             pltpu.VMEM((outer, waves), jnp.float32),
             pltpu.VMEM((outer, waves), jnp.float32),
-            pltpu.VMEM((used * rows, each_band), jnp.bfloat16),
-            pltpu.VMEM((used * rows, each_band), jnp.bfloat16),
             pltpu.VMEM((used * rows, INNER), jnp.float32),
             pltpu.VMEM((cycles, 2 * FIELDS, each_band), jnp.bfloat16),
             message, message, message,

time: 27.9 us -> 22.4 us (0.80)
  Pallas kernels: 27.8 us -> 22.2 us
    pallas_call x1, Pallas kernels: 23.4 us -> 19.8 us  [on_device(): pl.pallas_call(functools.partial(grid_kernel, points_dev, lev_count, spli...]
    pallas_call x1, Pallas kernels: 4.37 us -> 2.41 us  [on_device(): pl.pallas_call(functools.partial(direct_kernel, split), in_specs=[vmem, v...]
where the time goes in v2:
time: 22.4 us; the launch traced here: 22.3 us
  Pallas kernels  22.2 us (99%)
    pallas_call x1, Pallas kernels, on_device(): pl.pallas_call(functools.partial(grid_kernel, points_dev, lev_count, spli...  19.8 us
    pallas_call x1, Pallas kernels, on_device(): pl.pallas_call(functools.partial(direct_kernel, split), in_specs=[vmem, v...  2.41 us

profile of v2, /device:TPU:0, one launch (start us, length us, event | category | flops | bytes accessed | tf_op | source)
XLA Modules:
  0.0 22.3 jit_solution(3670846418110687252)
XLA Ops:
  0.0 19.8 %shard_map.73 = (f32[10,8,128]{2,1,0:T(8,128)S(1)}, s32[160,1]{1,0:T(8,128)S(1)}, bf16[160,8,2561]{2,1,0:T(8,128)(2,1)S(1)}) custom-call(s32[8]{0:T(128)} %length_hbm.1, f32[8]{0:T(128)} %weight_hbm.1, s32[1280]{0:T(1024)} %low_hbm.1, bf16[2,4,2564]{2,1,0:T(4,128)(2,1)} %bitcast.1, bf16[2,4,4]{2,1,0:T(4,128)(2,1)} %mixing_hbm.1, ...), custom_call_target="tpu_custom_call" | custom-call | tf_op jit(solution)/shard_map/pallas_call | solution.py:440
  19.9 2.4 %shard_map.74 = bf16[2,2,1,160,2561]{4,3,2,1,0:T(8,128)(2,1)} custom-call(s32[160,1]{1,0:T(8,128)S(1)} %get-tuple-element.8.limit_ref, f32[10,8,128]{2,1,0:T(8,128)S(1)} %get-tuple-element.9.coeff_ref, bf16[160,8,2561]{2,1,0:T(8,128)(2,1)S(1)} %get-tuple-element.10.leg_ref), custom_call_target="tpu_custom_call" | custom-call | tf_op jit(solution)/shard_map/pallas_call | solution.py:482

commit v3 on v2

--- a/solution.py
+++ b/solution.py
@@ -9,7 +9,8 @@
 
 TRUNC = 2559
 FIELDS = 2
-INNER = 256
+HALF = 128
+INNER = 2 * HALF
 VMEM_LIMIT = 32 << 20
 TWO_PI = 6.283185307179586
 
@@ -95,7 +96,7 @@
     points_dev, levs, split, length_hbm, weight_hbm, low_hbm, forcing_hbm, mixing_hbm, spec_hbm, leg_hbm,
     out_ref, limit_ref, leg_ref,
     length_ref, weight_ref, low_ref, forcing_ref, mixing_ref,
-    cos_tab, sin_tab, cos_out, sin_out, grid_ref,
+    cos_tab, sin_tab, cos_out, sin_out, grid_ref, force_ref,
     outgoing, incoming, partial, arrived, spec_vmem, four_ref, wave_ref,
     send_sem, recv_sem, send_back, recv_back, leg_sem, spec_sem, small_sem,
 ):
@@ -180,18 +181,20 @@
     mine = jnp.broadcast_to(wave_ref[pl.ds(band_id, 1), :].astype(jnp.float32), (8, lanes)).T
     limit_ref[...] = TRUNC + 1 - mine[: blocks * pairs, 0:1].astype(jnp.int32)
 
+    twice, inverse_twice = 2 * length, 0.5 * inverse_length
+
     def tables(c):
         span = pl.ds(pl.multiple_of(c * lanes, lanes), lanes)
         wave = wave_ref[pl.ds(c, 1), :]
         eight = lax.broadcasted_iota(jnp.int32, (8, lanes), 0)
-        c0, s0 = sincos(wave, eight, length, inverse_length)
-        c1, s1 = sincos(wave, eight * 8, length, inverse_length)
-        c2, s2 = sincos(wave, eight * 64, length, inverse_length)
+        c0, s0 = sincos(wave, eight * 2 + 1, twice, inverse_twice)
+        c1, s1 = sincos(wave, eight * 16, twice, inverse_twice)
+        c2, s2 = sincos(wave, eight * 128, twice, inverse_twice)
         steps = lax.broadcasted_iota(jnp.int32, (outer, lanes), 0)
-        c3, s3 = sincos(wave, base + steps * INNER, length, inverse_length)
+        c3, s3 = sincos(wave, 2 * base + INNER - 1 + steps * (2 * INNER), twice, inverse_twice)
         cos_out[:, span] = c3
         sin_out[:, span] = s3
-        for high in range(INNER // 64):
+        for high in range(HALF // 64):
             ch, sh = c2[high : high + 1], s2[high : high + 1]
             cj, sj = ch * c1 - sh * s1, ch * s1 + sh * c1
             for mid in range(8):
@@ -269,6 +272,27 @@
     incoming[me] = outgoing[band_id]
 
     pl.loop(early, bands)(tables)
+
+    def force_at(start):
+        stop = min(start + HALF, points_dev)
+        if stop <= start:
+            return jnp.zeros((rows, HALF), jnp.float32)
+        force = [forcing_ref[f, :, start:stop].astype(jnp.float32) for f in range(FIELDS)]
+        force = jnp.concatenate(force, axis=0)
+        if stop < start + HALF:
+            rest = jnp.zeros((rows, start + HALF - stop), jnp.float32)
+            force = jnp.concatenate([force, rest], axis=1)
+        return force
+
+    for copy in small[3:]:
+        copy.wait()
+    before = jnp.concatenate([force_at(a * INNER) for a in range(used)], axis=0)
+    turned = lax.broadcasted_iota(jnp.int32, (HALF, HALF), 0) + lax.broadcasted_iota(
+        jnp.int32, (HALF, HALF), 1
+    )
+    turned = jnp.where(turned == HALF - 1, 1.0, 0.0).astype(jnp.bfloat16)
+    force_ref[0] = jnp.concatenate([force_at(a * INNER + HALF) for a in range(used)], axis=0)
+    force_ref[1] = jnp.dot(before.astype(jnp.bfloat16), turned, preferred_element_type=jnp.float32)
 
     def wait_all(semaphore, buffer, count):
         most = buffer.at[pl.ds(0, count)]
@@ -305,9 +329,9 @@
             twist_im.append(-(re * so + im * co))
         twist_re = jnp.concatenate(twist_re, axis=0).astype(jnp.bfloat16)
         twist_im = jnp.concatenate(twist_im, axis=0).astype(jnp.bfloat16)
-        return lax.dot_general(
-            twist_re, cos_tab[:, span], contract, preferred_element_type=jnp.float32
-        ) + lax.dot_general(twist_im, sin_tab[:, span], contract, preferred_element_type=jnp.float32)
+        even = lax.dot_general(twist_re, cos_tab[:, span], contract, preferred_element_type=jnp.float32)
+        odd = lax.dot_general(twist_im, sin_tab[:, span], contract, preferred_element_type=jnp.float32)
+        return even, odd
 
     def wait_group(flips, own):
         group = toggled(band_id // near, flips, groups)
@@ -321,36 +345,41 @@
 
     if groups <= 8:
         these = [wait_group(flips, flips == 0) for flips in range(groups)]
-        grid = sum(synthesis(group) for group in these)
+        halves = [synthesis(group) for group in these]
+        even = sum(half[0] for half in halves)
+        odd = sum(half[1] for half in halves)
     else:
-        grid_ref[...] = synthesis(wait_group(0, True))
+        grid_ref[0], grid_ref[1] = synthesis(wait_group(0, True))
 
         @pl.loop(1, groups)
         def _(flips):
-            grid_ref[...] += synthesis(wait_group(flips, False))
-
-        grid = grid_ref[...]
-
-    for copy in small[3:]:
-        copy.wait()
-    lane = lax.broadcasted_iota(jnp.int32, (rows, INNER), 1)
+            half = synthesis(wait_group(flips, False))
+            grid_ref[0] += half[0]
+            grid_ref[1] += half[1]
+
+        even, odd = grid_ref[0], grid_ref[1]
+
+    lane = lax.broadcasted_iota(jnp.int32, (rows, HALF), 1)
     mixing = jnp.concatenate([mixing_ref[f].astype(jnp.float32) for f in range(FIELDS)], axis=0)
-    updated = []
-    for a in range(used):
-        point = a * INNER + lane
+
+    def physics(side, values, a):
+        point = a * INNER + (HALF - 1 - lane if side else HALF + lane)
         inside = (point < points_dev) & (base + point < length)
-        cell = jnp.where(inside, grid[a * rows : (a + 1) * rows], 0.0)
+        cell = jnp.where(inside, values, 0.0)
         product = (cell[:levs] * cell[levs:]).astype(jnp.bfloat16).astype(jnp.float32)
-        span = slice(a * INNER, min((a + 1) * INNER, points_dev))
-        force = jnp.concatenate([forcing_ref[f, :, span].astype(jnp.float32) for f in range(FIELDS)], axis=0)
-        if force.shape[1] < INNER:
-            rest = jnp.zeros((rows, INNER - force.shape[1]), jnp.float32)
-            force = jnp.concatenate([force, rest], axis=1)
-        total = cell + force
+        total = cell + force_ref[side, a * rows : (a + 1) * rows]
         for l2 in range(levs):
             total = total + mixing[:, l2 : l2 + 1] * product[l2 : l2 + 1]
-        updated.append(jnp.where(inside, total, 0.0))
-    updated = jnp.concatenate(updated, axis=0).astype(jnp.bfloat16)
+        return jnp.where(inside, total, 0.0)
+
+    sums, gaps = [], []
+    for a in range(used):
+        at = slice(a * rows, (a + 1) * rows)
+        after, before = physics(0, even[at] + odd[at], a), physics(1, even[at] - odd[at], a)
+        sums.append(after + before)
+        gaps.append(after - before)
+    sums = jnp.concatenate(sums, axis=0).astype(jnp.bfloat16)
+    gaps = jnp.concatenate(gaps, axis=0).astype(jnp.bfloat16)
 
     send_partial = send(
         lambda band, lev: partial.at[band * levs + lev], arrived, send_back, recv_back
@@ -359,8 +388,8 @@
     def analysis(flips):
         group = toggled(band_id // near, flips, groups)
         span = span_of(group)
-        cos_part = jnp.dot(updated, cos_tab[:, span], preferred_element_type=jnp.float32)
-        sin_part = jnp.dot(updated, sin_tab[:, span], preferred_element_type=jnp.float32)
+        cos_part = jnp.dot(sums, cos_tab[:, span], preferred_element_type=jnp.float32)
+        sin_part = jnp.dot(gaps, sin_tab[:, span], preferred_element_type=jnp.float32)
         re = jnp.zeros((rows, near * lanes), jnp.float32)
         im = jnp.zeros((rows, near * lanes), jnp.float32)
         for a in range(used):
@@ -401,14 +430,14 @@
     send_group(0)
 
     wait_all(recv_back, arrived, slots - 1)
-    sums = []
+    levels_sum = []
     for j in range(cycles):
         total = arrived[j * levs].astype(jnp.float32)
         for lev in range(1, levs):
             total = total + arrived[j * levs + lev].astype(jnp.float32)
-        sums.append(total)
+        levels_sum.append(total)
     for k in range(4):
-        side = jnp.concatenate([total[k : k + 1] for total in sums], axis=0)
+        side = jnp.concatenate([total[k : k + 1] for total in levels_sum], axis=0)
         for h in range(2):
             for i in range(blocks):
                 at, lane = (4 * h + k) * pairs, (h * blocks + i) * pairs
@@ -452,11 +481,12 @@
             pltpu.VMEM(pair_wave.shape, jnp.int32),
             pltpu.VMEM(force.shape, jnp.bfloat16),
             pltpu.VMEM(mixing.shape, jnp.bfloat16),
-            pltpu.VMEM((INNER, waves), jnp.bfloat16),
-            pltpu.VMEM((INNER, waves), jnp.bfloat16),
+            pltpu.VMEM((HALF, waves), jnp.bfloat16),
+            pltpu.VMEM((HALF, waves), jnp.bfloat16),
             pltpu.VMEM((outer, waves), jnp.float32),
             pltpu.VMEM((outer, waves), jnp.float32),
-            pltpu.VMEM((used * rows, INNER), jnp.float32),
+            pltpu.VMEM((2, used * rows, HALF), jnp.float32),
+            pltpu.VMEM((2, used * rows, HALF), jnp.float32),
             pltpu.VMEM((cycles, 2 * FIELDS, each_band), jnp.bfloat16),
             message, message, message,
             pltpu.VMEM(spectral.shape, jnp.bfloat16),

time: 22.4 us -> 21.5 us (0.960)
  Pallas kernels: 22.2 us -> 21.3 us
    pallas_call x1, Pallas kernels: 19.8 us -> 18.9 us  [on_device(): pl.pallas_call(functools.partial(grid_kernel, points_dev, lev_count, spli...]
where the time goes in v3:
time: 21.5 us; the launch traced here: 21.3 us
  Pallas kernels  21.3 us (99%)
    pallas_call x1, Pallas kernels, on_device(): pl.pallas_call(functools.partial(grid_kernel, points_dev, lev_count, spli...  18.9 us
    pallas_call x1, Pallas kernels, on_device(): pl.pallas_call(functools.partial(direct_kernel, split), in_specs=[vmem, v...  2.41 us

profile of v3, /device:TPU:0, one launch (start us, length us, event | category | flops | bytes accessed | tf_op | source)
XLA Modules:
  0.0 21.3 jit_solution(14441472482783587273)
XLA Ops:
  0.0 18.9 %shard_map.73 = (f32[10,8,128]{2,1,0:T(8,128)S(1)}, s32[160,1]{1,0:T(8,128)S(1)}, bf16[160,8,2561]{2,1,0:T(8,128)(2,1)S(1)}) custom-call(s32[8]{0:T(128)} %length_hbm.1, f32[8]{0:T(128)} %weight_hbm.1, s32[1280]{0:T(1024)} %low_hbm.1, bf16[2,4,2564]{2,1,0:T(4,128)(2,1)} %bitcast.1, bf16[2,4,4]{2,1,0:T(4,128)(2,1)} %mixing_hbm.1, ...), custom_call_target="tpu_custom_call" | custom-call | tf_op jit(solution)/shard_map/pallas_call | solution.py:469
  18.9 2.4 %shard_map.74 = bf16[2,2,1,160,2561]{4,3,2,1,0:T(8,128)(2,1)} custom-call(s32[160,1]{1,0:T(8,128)S(1)} %get-tuple-element.8.limit_ref, f32[10,8,128]{2,1,0:T(8,128)S(1)} %get-tuple-element.9.coeff_ref, bf16[160,8,2561]{2,1,0:T(8,128)(2,1)S(1)} %get-tuple-element.10.leg_ref), custom_call_target="tpu_custom_call" | custom-call | tf_op jit(solution)/shard_map/pallas_call | solution.py:512

commit v4 on v3

--- a/solution.py
+++ b/solution.py
@@ -12,6 +12,8 @@
 HALF = 128
 INNER = 2 * HALF
 VMEM_LIMIT = 32 << 20
+STEP = 2
+CHUNK = 256
 TWO_PI = 6.283185307179586
 
 
@@ -67,7 +69,8 @@
         )
 
     mask = diagonal(pairs, cycles)
-    column = split + lax.broadcasted_iota(jnp.int32, (pairs, packed - split), 1)
+    whole = packed // 128 * 128
+    column = split + lax.broadcasted_iota(jnp.int32, (pairs, whole - split), 1)
     half = 4 * pairs
 
     @pl.loop(0, blocks, unroll=blocks <= 10)
@@ -75,17 +78,26 @@
         part = pl.ds(pl.multiple_of(i * pairs, pairs), pairs)
         wide = jnp.broadcast_to(coeff_ref[pl.ds(i, 1)], (pairs, cycles, 8 * pairs))
         wide = jnp.where(mask, wide, 0.0).reshape(pairs * cycles, 8 * pairs)
-        wide = wide.T.astype(jnp.bfloat16)
+        wide = wide.astype(jnp.bfloat16).astype(jnp.float32)
         lower = column < limit_ref[part]
         leg = leg_ref[part].reshape(pairs * cycles, packed)
+        beyond = [
+            jnp.sum(wide * leg[:, at : at + 1].astype(jnp.float32), axis=0, keepdims=True)
+            for at in range(whole, packed)
+        ]
+        beyond.append(jnp.zeros((8 - len(beyond), 8 * pairs), jnp.float32))
+        wide = jnp.concatenate([wide] + beyond, axis=0).T
+        beyond = wide[half:, pairs * cycles : pairs * cycles + packed - whole].astype(jnp.bfloat16)
+        wide = wide[:, : pairs * cycles].astype(jnp.bfloat16)
         left = jnp.dot(wide[:half], leg[:, :split], preferred_element_type=jnp.float32)
-        right = jnp.dot(wide, leg[:, split:], preferred_element_type=jnp.float32)
+        right = jnp.dot(wide, leg[:, split:whole], preferred_element_type=jnp.float32)
         for s in range(2):
             for f in range(FIELDS):
                 at = (s * FIELDS + f) * pairs
                 out_vmem[s, f, 0, part, :split] = left[at : at + pairs].astype(jnp.bfloat16)
                 low, high = right[at : at + pairs], right[half + at : half + at + pairs]
-                out_vmem[s, f, 0, part, split:] = jnp.where(lower, low, high).astype(jnp.bfloat16)
+                out_vmem[s, f, 0, part, split:whole] = jnp.where(lower, low, high).astype(jnp.bfloat16)
+                out_vmem[s, f, 0, part, whole:] = beyond[at : at + pairs]
         write(i).start()
 
     for i in range(blocks):
@@ -138,7 +150,7 @@
     base = lev_id * points_dev
     barrier = pltpu.get_barrier_semaphore()
 
-    def each_peer(act):
+    def each_peer(act, midway=None):
         def of_band(flips, skip):
             band = toggled(band_id, flips, bands)
             for turn in range(levs - 1, skip - 1, -1):
@@ -147,23 +159,30 @@
         if slots <= 64:
             for flips in range(bands - 1, 0, -1):
                 of_band(flips, 0)
+                if midway and flips == bands // 2:
+                    midway()
         else:
             @pl.loop(1, bands)
             def _(step):
                 of_band(bands - step, 0)
+
+            if midway:
+                midway()
         of_band(0, 1)
+
+    def read_all():
+        for i in range(blocks):
+            read_spec(i).start()
+            read_leg(i).start()
+        for copy in small[3:]:
+            copy.start()
 
     each_peer(
         lambda band, lev: pl.semaphore_signal(
             barrier, inc=1, device_id={"band": band, "lev": lev}, device_id_type=pl.DeviceIdType.MESH
-        )
+        ),
+        read_all,
     )
-
-    for i in range(blocks):
-        read_spec(i).start()
-        read_leg(i).start()
-    for copy in small[3:]:
-        copy.start()
 
     for at, copy in enumerate(small[:3]):
         copy.wait()
@@ -321,12 +340,12 @@
         re = jnp.concatenate([cells[lev][f : f + 1] for f, lev in order], axis=0)
         im = jnp.concatenate([cells[lev][FIELDS + f : FIELDS + f + 1] for f, lev in order], axis=0)
         re = jnp.where(live, re * gain, 0.0)
-        im = jnp.where(live, im * gain, 0.0)
+        im = jnp.where(live, im * -gain, 0.0)
         twist_re, twist_im = [], []
         for a in range(used):
             co, so = cos_out[a : a + 1, span], sin_out[a : a + 1, span]
-            twist_re.append(re * co - im * so)
-            twist_im.append(-(re * so + im * co))
+            twist_re.append(re * co + im * so)
+            twist_im.append(im * co - re * so)
         twist_re = jnp.concatenate(twist_re, axis=0).astype(jnp.bfloat16)
         twist_im = jnp.concatenate(twist_im, axis=0).astype(jnp.bfloat16)
         even = lax.dot_general(twist_re, cos_tab[:, span], contract, preferred_element_type=jnp.float32)
@@ -344,10 +363,13 @@
         return group
 
     if groups <= 8:
-        these = [wait_group(flips, flips == 0) for flips in range(groups)]
-        halves = [synthesis(group) for group in these]
-        even = sum(half[0] for half in halves)
-        odd = sum(half[1] for half in halves)
+        even, odd = 0.0, 0.0
+        for last in range(groups - 1, -1, -STEP):
+            these = range(last, max(last - STEP, -1), -1)
+            these = [wait_group(flips, flips == 0) for flips in these]
+            for group in these:
+                half = synthesis(group)
+                even, odd = even + half[0], odd + half[1]
     else:
         grid_ref[0], grid_ref[1] = synthesis(wait_group(0, True))
 
@@ -385,49 +407,41 @@
         lambda band, lev: partial.at[band * levs + lev], arrived, send_back, recv_back
     )
 
-    def analysis(flips):
-        group = toggled(band_id // near, flips, groups)
-        span = span_of(group)
-        cos_part = jnp.dot(sums, cos_tab[:, span], preferred_element_type=jnp.float32)
-        sin_part = jnp.dot(gaps, sin_tab[:, span], preferred_element_type=jnp.float32)
-        re = jnp.zeros((rows, near * lanes), jnp.float32)
-        im = jnp.zeros((rows, near * lanes), jnp.float32)
-        for a in range(used):
-            co, so = cos_out[a : a + 1, span], sin_out[a : a + 1, span]
-            cp, sp = cos_part[a * rows : (a + 1) * rows], sin_part[a * rows : (a + 1) * rows]
-            re = re + (cp * co - sp * so)
-            im = im + (cp * so + sp * co)
-        scale = jnp.concatenate([factor] * near, axis=1)
-        keep = 2 * waves_of(group) < length
-        re = jnp.where(keep, re * scale, 0.0)
-        im = jnp.where(keep, im * -scale, 0.0)
+    def analysis(band):
+        pieces = []
+        for start in range(0, lanes, CHUNK):
+            size = min(CHUNK, lanes - start)
+            span = pl.ds(pl.multiple_of(band * lanes + start, 128), size)
+            cos_part = jnp.dot(sums, cos_tab[:, span], preferred_element_type=jnp.float32)
+            sin_part = jnp.dot(gaps, sin_tab[:, span], preferred_element_type=jnp.float32)
+            re = jnp.zeros((rows, size), jnp.float32)
+            im = jnp.zeros((rows, size), jnp.float32)
+            for a in range(used):
+                co, so = cos_out[a : a + 1, span], sin_out[a : a + 1, span]
+                cp, sp = cos_part[a * rows : (a + 1) * rows], sin_part[a * rows : (a + 1) * rows]
+                re = re + (cp * co - sp * so)
+                im = im + (cp * so + sp * co)
+            pieces.append((re, im))
+        re, im = (jnp.concatenate(side, axis=1) for side in zip(*pieces))
+        keep = 2 * wave_ref[pl.ds(band, 1), :] < length
+        re = jnp.where(keep, re * factor, 0.0)
+        im = jnp.where(keep, im * -factor, 0.0)
         for lev in range(levs):
             picks = [side[f * levs + lev : f * levs + lev + 1] for side in (re, im) for f in range(FIELDS)]
-            picks = jnp.concatenate(picks, axis=0).astype(jnp.bfloat16)
-            for at in range(near):
-                partial[(group * near + at) * levs + lev] = picks[:, at * lanes : (at + 1) * lanes]
-
-    def send_group(flips):
-        group = toggled(band_id // near, flips, groups)
-        for at in range(near - 1, -1, -1):
-            own = isinstance(flips, int) and flips == 0 and at == 0
-            band = group * near + (band_id + at) % near
-            for turn in range(levs - 1, 0 if own else -1, -1):
-                send_partial(band, (lev_id + turn) % levs)
-
-    analysis(groups - 1)
-    if groups <= 8:
-        for flips in range(groups - 2, -1, -1):
-            analysis(flips)
-            send_group(flips + 1)
+            partial[band * levs + lev] = jnp.concatenate(picks, axis=0).astype(jnp.bfloat16)
+
+    def serve(band):
+        analysis(band)
+        for turn in range(levs - 1, 0, -1):
+            send_partial(band, (lev_id + turn) % levs)
+        pl.when(band != band_id)(functools.partial(send_partial, band, lev_id))
+
+    if bands <= 8:
+        for band in range(bands):
+            serve(band)
     else:
-        @pl.loop(1, groups)
-        def _(step):
-            analysis(groups - 1 - step)
-            send_group(groups - step)
-
+        pl.loop(0, bands)(serve)
     arrived[me] = partial[me]
-    send_group(0)
 
     wait_all(recv_back, arrived, slots - 1)
     levels_sum = []

time: 21.5 us -> 20.4 us (0.949)
  Pallas kernels: 21.3 us -> 20.2 us
    pallas_call x1, Pallas kernels: 18.9 us -> 17.8 us  [on_device(): pl.pallas_call(functools.partial(grid_kernel, points_dev, lev_count, spli...]
where the time goes in v4:
time: 20.4 us; the launch traced here: 20.2 us
  Pallas kernels  20.2 us (99%)
    pallas_call x1, Pallas kernels, on_device(): pl.pallas_call(functools.partial(grid_kernel, points_dev, lev_count, spli...  17.8 us
    pallas_call x1, Pallas kernels, on_device(): pl.pallas_call(functools.partial(direct_kernel, split), in_specs=[vmem, v...  2.37 us

profile of v4, /device:TPU:0, one launch (start us, length us, event | category | flops | bytes accessed | tf_op | source)
XLA Modules:
  0.0 20.2 jit_solution(18171357819957505824)
XLA Ops:
  0.0 17.8 %shard_map.73 = (f32[10,8,128]{2,1,0:T(8,128)S(1)}, s32[160,1]{1,0:T(8,128)S(1)}, bf16[160,8,2561]{2,1,0:T(8,128)(2,1)S(1)}) custom-call(s32[8]{0:T(128)} %length_hbm.1, f32[8]{0:T(128)} %weight_hbm.1, s32[1280]{0:T(1024)} %low_hbm.1, bf16[2,4,2564]{2,1,0:T(4,128)(2,1)} %bitcast.1, bf16[2,4,4]{2,1,0:T(4,128)(2,1)} %mixing_hbm.1, ...), custom_call_target="tpu_custom_call" | custom-call | tf_op jit(solution)/shard_map/pallas_call | solution.py:483
  17.8 2.4 %shard_map.74 = bf16[2,2,1,160,2561]{4,3,2,1,0:T(8,128)(2,1)} custom-call(s32[160,1]{1,0:T(8,128)S(1)} %get-tuple-element.8.limit_ref, f32[10,8,128]{2,1,0:T(8,128)S(1)} %get-tuple-element.9.coeff_ref, bf16[160,8,2561]{2,1,0:T(8,128)(2,1)S(1)} %get-tuple-element.10.leg_ref), custom_call_target="tpu_custom_call" | custom-call | tf_op jit(solution)/shard_map/pallas_call | solution.py:526
